TPU v7x, 128 devices: a whole 4x4x4 slice. The times are simulated.
128 devices in a mesh: req: 32 (over x, z, core), tp: 4 (over y).
Axes of the slice: x: 4, y: 4, z: 4, core: 2. Of those that a mesh axis runs over, the one named last changes fastest.
Arguments:
- hidden_states: bfloat16 [8192, 2048], P('req'), may hold values from -30 to 30
- norm_gain: float32 [2048], replicated, may hold values from 0.5 to 1.5
- head: bfloat16 [2048, 98304], P(None, ('req', 'tp')), may hold values from -1 to 1
- target_ids: int32 [8192], P('req'), may hold values from 0 to 98303
- lengths: int32 [32], P('req'), may hold values from 32 to 256, as said below
Outputs:
- token_logprob: float32 [8192], P('req')
- token_entropy: float32 [8192], P('req')
- seq_mean_logprob: float32 [32], P('req')
- seq_top_logit: float32 [32], P('req')
Inputs may be any that keep to these rules, and one draw needn't show every extreme that they name: `lengths`: each completion has at least 32 and at most 256 live slots; some completion has exactly 256.
All inputs are finite; a program needn't handle non-finite values.
Results may differ from a plain program's by a relative error of at most 0.0018.
Values may be sent and summed in bfloat16 or wider, within the bound.
A program may use at most 128 MiB of HBM per device.

v0:
```python
import math

import jax
import jax.numpy as jnp
from jax import lax
from jax.sharding import PartitionSpec as P


def combined_all(value, axis, combine):
    everything = jax.tree.map(lambda part: lax.all_gather(part, axis), value)
    leading = jax.tree.map(lambda part: part[0], everything)

    def turn(k, so_far):
        return combine(so_far, jax.tree.map(lambda part: part[k], everything))

    return lax.fori_loop(1, lax.axis_size(axis), turn, leading)


def combine(first, second):
    top = jnp.maximum(first[0], second[0])
    left = jnp.exp(first[0] - top)
    right = jnp.exp(second[0] - top)
    return (
        top,
        first[1] * left + second[1] * right,
        first[2] * left + second[2] * right,
        first[3] + second[3],
    )


def block_stats(block, target, matrix, vocab_ids):
    logits = jnp.dot(block, matrix, preferred_element_type=jnp.float32)
    top = jnp.max(logits, axis=-1)
    shifted = jnp.exp(logits - top[:, None])
    weight_sum = jnp.sum(shifted, axis=-1)
    weighted = jnp.sum(shifted * logits, axis=-1)
    hit = vocab_ids == target[:, None]
    picked = jnp.sum(jnp.where(hit, logits, 0.0), axis=-1)
    return (top, weight_sum, weighted, picked)


def blocked_stats(block, target, matrix, vocab_ids):
    count = block.shape[0]
    step = math.gcd(count, 512)
    stats = lax.map(
        lambda a: block_stats(a[0], a[1], matrix, vocab_ids),
        (block.reshape(count // step, step, block.shape[1]), target.reshape(count // step, step)),
    )
    return tuple((s.reshape(-1) for s in stats))


def per_device(hidden_states, norm_gain, head, target_ids, lengths):
    feats = hidden_states.astype(jnp.float32)
    scale = lax.rsqrt(jnp.mean(feats * feats, axis=-1, keepdims=True) + 1e-06)
    normed = (feats * scale * norm_gain).astype(jnp.bfloat16)
    rows = hidden_states.shape[0]
    vdev = head.shape[1]
    n_req = lax.axis_size("req")
    n_tp = lax.axis_size("tp")
    my_req = lax.axis_index("req")
    vbase = (my_req * n_tp + lax.axis_index("tp")) * vdev
    columns = lax.broadcasted_iota(jnp.int32, (1, vdev), 1)
    own_vocab = columns + vbase
    block = lax.all_gather(normed, "req", axis=0, tiled=True)
    target = lax.all_gather(target_ids, "req", axis=0, tiled=True)
    stats = blocked_stats(block, target, head, own_vocab)
    gathered = tuple((new for new in stats))
    shaped = tuple((s.reshape(n_req, rows) for s in gathered))
    arrived = (
        lax.all_to_all(shaped[0], "req", split_axis=0, concat_axis=0, tiled=True),
        lax.all_to_all(shaped[1], "req", split_axis=0, concat_axis=0, tiled=True),
        lax.all_to_all(shaped[2], "req", split_axis=0, concat_axis=0, tiled=True),
        lax.all_to_all(shaped[3], "req", split_axis=0, concat_axis=0, tiled=True),
    )
    top = jnp.max(arrived[0], axis=0)
    factor = jnp.exp(arrived[0] - top[None, :])
    own = (
        top,
        jnp.sum(arrived[1] * factor, axis=0),
        jnp.sum(arrived[2] * factor, axis=0),
        jnp.sum(arrived[3], axis=0),
    )
    merged = combined_all((own[0], own[1], own[2], own[3]), "tp", combine)
    top, weight_sum, weighted, picked = merged
    log_norm = top + jnp.log(weight_sum)
    live = jnp.arange(rows, dtype=jnp.int32) < lengths[0]
    logprob = jnp.where(live, picked - log_norm, jnp.float32(0.0))
    entropy = jnp.where(live, log_norm - weighted / weight_sum, jnp.float32(0.0))
    mean_lp = (jnp.sum(logprob) / lengths[0].astype(jnp.float32)).reshape(1)
    top_live = jnp.max(jnp.where(live, top, jnp.float32(-1e30))).reshape(1)
    return (logprob, entropy, mean_lp, top_live)


def solution(mesh):
    in_specs = (P("req", None), P(), P(None, ("req", "tp")), P("req"), P("req"))
    out_specs = (P("req"), P("req"), P("req"), P("req"))
    return jax.shard_map(
        per_device, mesh=mesh, in_specs=in_specs, out_specs=out_specs, check_vma=False
    )
```

profile of v0, /device:TPU:0, one launch (start us, length us, event | category | flops | bytes accessed | tf_op | source)
XLA Modules:
  0.0 282.9 jit_solution(8951670508299853403)
XLA Ops:
  11.5 25.6 %all-gather.4 = s32[32,1,256]{2,1,0:T(1,128)S(1)} all-gather(s32[1,1,256]{2,1,0:T(1,128)S(1)} %bitcast.102), channel_id=1, replica_groups=mesh['req'=32,'tp'=4] {'req'}, dimensions={0}, use_global_device_ids=true | all-gather | bytes 33792 | tf_op jit(solution)/shard_map/all_gather | solution.py:65
  37.2 90.9 %all-gather.11.cloned.1.call-done = bf16[8192,2048]{1,0:T(8,128)(2,1)} async-done(((bf16[256,2048]{1,0:T(8,128)(2,1)}), bf16[8192,2048]{1,0:T(8,128)(2,1)}) %all-gather.11.cloned.1.call-update) | async-done | bytes 33554448 | tf_op jit(solution)/shard_map/all_gather | solution.py:64
  128.1 72.3 %while.39 = (s32[]{:T(128)}, f32[16,512]{1,0:T(8,128)S(1)}, f32[16,512]{1,0:T(8,128)S(1)}, f32[16,512]{1,0:T(8,128)S(1)}, f32[16,512]{1,0:T(8,128)S(1)}, /*index...) while((s32[]{:T(128)}, f32[16,512]{1,0:T(8,128)S(1)}, ...), condition=%wide.region_6.7_spmd.clone, body=%wide.region_1.6_spmd.clone.sunk | while | flops 1613757184 | bytes 8428165 | solution.py:45
  132.6 3.5 %fusion.19 = (f32[512]{0:T(512)S(1)}, f32[512,768]{1,0:T(8,128)S(1)}) fusion(bf16[2048,768]{1,0:T(8,128)(2,1)S(1)} %get-tuple-element.519, bf16[16,512,2048]{2,1,0:T(8,128)(2,1)} %get-tuple-element.518, s32[]{:T(128)} %get-tuple-element.502), kind=kOutput, calls=%fused_computation.41.clone.1 | convolution fusion | flops 1611005440 | bytes 6818304 | tf_op jit(solution)/shard_map/while/body/eval_jaxpr/dot_general | solution.py:32
  141.6 3.5 %fusion.19 = (f32[512]{0:T(512)S(1)}, f32[512,768]{1,0:T(8,128)S(1)}) fusion(bf16[2048,768]{1,0:T(8,128)(2,1)S(1)} %get-tuple-element.519, bf16[16,512,2048]{2,1,0:T(8,128)(2,1)} %get-tuple-element.518, s32[]{:T(128)} %get-tuple-element.502), kind=kOutput, calls=%fused_computation.41.clone.1 | convolution fusion | flops 1611005440 | bytes 6818304 | tf_op jit(solution)/shard_map/while/body/eval_jaxpr/dot_general | solution.py:32
  146.2 3.5 %fusion.19 = (f32[512]{0:T(512)S(1)}, f32[512,768]{1,0:T(8,128)S(1)}) fusion(bf16[2048,768]{1,0:T(8,128)(2,1)S(1)} %get-tuple-element.519, bf16[16,512,2048]{2,1,0:T(8,128)(2,1)} %get-tuple-element.518, s32[]{:T(128)} %get-tuple-element.502), kind=kOutput, calls=%fused_computation.41.clone.1 | convolution fusion | flops 1611005440 | bytes 6818304 | tf_op jit(solution)/shard_map/while/body/eval_jaxpr/dot_general | solution.py:32
  150.7 3.5 %fusion.19 = (f32[512]{0:T(512)S(1)}, f32[512,768]{1,0:T(8,128)S(1)}) fusion(bf16[2048,768]{1,0:T(8,128)(2,1)S(1)} %get-tuple-element.519, bf16[16,512,2048]{2,1,0:T(8,128)(2,1)} %get-tuple-element.518, s32[]{:T(128)} %get-tuple-element.502), kind=kOutput, calls=%fused_computation.41.clone.1 | convolution fusion | flops 1611005440 | bytes 6818304 | tf_op jit(solution)/shard_map/while/body/eval_jaxpr/dot_general | solution.py:32
  159.7 3.5 %fusion.19 = (f32[512]{0:T(512)S(1)}, f32[512,768]{1,0:T(8,128)S(1)}) fusion(bf16[2048,768]{1,0:T(8,128)(2,1)S(1)} %get-tuple-element.519, bf16[16,512,2048]{2,1,0:T(8,128)(2,1)} %get-tuple-element.518, s32[]{:T(128)} %get-tuple-element.502), kind=kOutput, calls=%fused_computation.41.clone.1 | convolution fusion | flops 1611005440 | bytes 6818304 | tf_op jit(solution)/shard_map/while/body/eval_jaxpr/dot_general | solution.py:32
  168.8 3.5 %fusion.19 = (f32[512]{0:T(512)S(1)}, f32[512,768]{1,0:T(8,128)S(1)}) fusion(bf16[2048,768]{1,0:T(8,128)(2,1)S(1)} %get-tuple-element.519, bf16[16,512,2048]{2,1,0:T(8,128)(2,1)} %get-tuple-element.518, s32[]{:T(128)} %get-tuple-element.502), kind=kOutput, calls=%fused_computation.41.clone.1 | convolution fusion | flops 1611005440 | bytes 6818304 | tf_op jit(solution)/shard_map/while/body/eval_jaxpr/dot_general | solution.py:32
  173.3 3.5 %fusion.19 = (f32[512]{0:T(512)S(1)}, f32[512,768]{1,0:T(8,128)S(1)}) fusion(bf16[2048,768]{1,0:T(8,128)(2,1)S(1)} %get-tuple-element.519, bf16[16,512,2048]{2,1,0:T(8,128)(2,1)} %get-tuple-element.518, s32[]{:T(128)} %get-tuple-element.502), kind=kOutput, calls=%fused_computation.41.clone.1 | convolution fusion | flops 1611005440 | bytes 6818304 | tf_op jit(solution)/shard_map/while/body/eval_jaxpr/dot_general | solution.py:32
  177.8 3.5 %fusion.19 = (f32[512]{0:T(512)S(1)}, f32[512,768]{1,0:T(8,128)S(1)}) fusion(bf16[2048,768]{1,0:T(8,128)(2,1)S(1)} %get-tuple-element.519, bf16[16,512,2048]{2,1,0:T(8,128)(2,1)} %get-tuple-element.518, s32[]{:T(128)} %get-tuple-element.502), kind=kOutput, calls=%fused_computation.41.clone.1 | convolution fusion | flops 1611005440 | bytes 6818304 | tf_op jit(solution)/shard_map/while/body/eval_jaxpr/dot_general | solution.py:32
  186.8 3.5 %fusion.19 = (f32[512]{0:T(512)S(1)}, f32[512,768]{1,0:T(8,128)S(1)}) fusion(bf16[2048,768]{1,0:T(8,128)(2,1)S(1)} %get-tuple-element.519, bf16[16,512,2048]{2,1,0:T(8,128)(2,1)} %get-tuple-element.518, s32[]{:T(128)} %get-tuple-element.502), kind=kOutput, calls=%fused_computation.41.clone.1 | convolution fusion | flops 1611005440 | bytes 6818304 | tf_op jit(solution)/shard_map/while/body/eval_jaxpr/dot_general | solution.py:32
  195.9 3.5 %fusion.19 = (f32[512]{0:T(512)S(1)}, f32[512,768]{1,0:T(8,128)S(1)}) fusion(bf16[2048,768]{1,0:T(8,128)(2,1)S(1)} %get-tuple-element.519, bf16[16,512,2048]{2,1,0:T(8,128)(2,1)} %get-tuple-element.518, s32[]{:T(128)} %get-tuple-element.502), kind=kOutput, calls=%fused_computation.41.clone.1 | convolution fusion | flops 1611005440 | bytes 6818304 | tf_op jit(solution)/shard_map/while/body/eval_jaxpr/dot_general | solution.py:32
  201.0 5.2 %all-to-all-start = ((f32[32,1,256]{2,1,0:T(1,128)}), f32[32,1,256]{2,1,0:T(1,128)S(1)}, u32[]{:S(2)}, u32[]{:S(2)}) async-start(f32[32,1,256]{2,1,0:T(1,128)} %all_to_all.30), calls=%async_computation | async-start | bytes 65536 | tf_op jit(solution)/shard_map/all_to_all | solution.py:70
  206.9 6.8 %all-to-all-done = f32[32,1,256]{2,1,0:T(1,128)S(1)} async-done(((f32[32,1,256]{2,1,0:T(1,128)}), f32[32,1,256]{2,1,0:T(1,128)S(1)}, u32[]{:S(2)}, u32[]{:S(2)}) %all-to-all-start) | async-done | bytes 32800 | tf_op jit(solution)/shard_map/all_to_all | solution.py:70
  213.6 3.8 %all-to-all-start.1 = ((f32[32,1,256]{2,1,0:T(1,128)}), f32[32,1,256]{2,1,0:T(1,128)S(1)}, u32[]{:S(2)}, u32[]{:S(2)}) async-start(f32[32,1,256]{2,1,0:T(1,128)} %all_to_all.32), calls=%async_computation.1 | async-start | bytes 65536 | tf_op jit(solution)/shard_map/all_to_all | solution.py:71
  218.1 6.8 %all-to-all-done.1 = f32[32,1,256]{2,1,0:T(1,128)S(1)} async-done(((f32[32,1,256]{2,1,0:T(1,128)}), f32[32,1,256]{2,1,0:T(1,128)S(1)}, u32[]{:S(2)}, u32[]{:S(2)}) %all-to-all-start.1) | async-done | bytes 32800 | tf_op jit(solution)/shard_map/all_to_all | solution.py:71
  224.9 3.9 %all-to-all-start.2 = ((f32[32,1,256]{2,1,0:T(1,128)}), f32[32,1,256]{2,1,0:T(1,128)S(1)}, u32[]{:S(2)}, u32[]{:S(2)}) async-start(f32[32,1,256]{2,1,0:T(1,128)} %all_to_all.36), calls=%async_computation.2 | async-start | bytes 65536 | tf_op jit(solution)/shard_map/all_to_all | solution.py:72
  230.1 6.1 %all-to-all-done.2 = f32[32,1,256]{2,1,0:T(1,128)S(1)} async-done(((f32[32,1,256]{2,1,0:T(1,128)}), f32[32,1,256]{2,1,0:T(1,128)S(1)}, u32[]{:S(2)}, u32[]{:S(2)}) %all-to-all-start.2) | async-done | bytes 32800 | tf_op jit(solution)/shard_map/all_to_all | solution.py:72
  236.2 3.8 %all-to-all-start.3 = ((f32[32,1,256]{2,1,0:T(1,128)}), f32[32,1,256]{2,1,0:T(1,128)S(1)}, u32[]{:S(2)}, u32[]{:S(2)}) async-start(f32[32,1,256]{2,1,0:T(1,128)} %all_to_all.39), calls=%async_computation.3 | async-start | bytes 65536 | tf_op jit(solution)/shard_map/all_to_all | solution.py:73
  240.1 9.7 %all-gather.6 = f32[4,1,256]{2,1,0:T(1,128)S(1)} all-gather(f32[1,1,256]{2,1,0:T(1,128)S(1)} %bitcast.100), channel_id=3, replica_groups=mesh['req'=32,'tp'=4] {'tp'}, dimensions={0}, use_global_device_ids=true | all-gather | bytes 5120 | tf_op jit(solution)/shard_map/all_gather | solution.py:10
  249.8 7.0 %all-gather.7 = f32[4,1,256]{2,1,0:T(1,128)S(1)} all-gather(f32[1,1,256]{2,1,0:T(1,128)S(1)} %bitcast.99), channel_id=4, replica_groups=mesh['req'=32,'tp'=4] {'tp'}, dimensions={0}, use_global_device_ids=true | all-gather | bytes 5120 | tf_op jit(solution)/shard_map/all_gather | solution.py:10
  256.8 9.0 %all-gather.5 = f32[4,1,256]{2,1,0:T(1,128)S(1)} all-gather(f32[1,1,256]{2,1,0:T(1,128)S(1)} %bitcast.98), channel_id=2, replica_groups=mesh['req'=32,'tp'=4] {'tp'}, dimensions={0}, use_global_device_ids=true | all-gather | bytes 5120 | tf_op jit(solution)/shard_map/all_gather | solution.py:10
  265.8 7.0 %all-gather.8 = f32[4,1,256]{2,1,0:T(1,128)S(1)} all-gather(f32[1,1,256]{2,1,0:T(1,128)S(1)} %bitcast.101), channel_id=5, replica_groups=mesh['req'=32,'tp'=4] {'tp'}, dimensions={0}, use_global_device_ids=true | all-gather | bytes 5120 | tf_op jit(solution)/shard_map/all_gather | solution.py:10
  (169 shorter events, 45.5 us)
Async XLA Ops:
  7.2 4.3 %copy-start = (s32[256]{0:T(256)S(1)}, s32[256]{0:T(256)}, u32[]{:S(2)}) copy-start(s32[256]{0:T(256)} %param.12) | copy-start | bytes 3076
  7.2 120.9 %copy-start.1 = (bf16[2048,768]{1,0:T(8,128)(2,1)S(1)}, bf16[2048,768]{1,0:T(8,128)(2,1)}, u32[]{:S(2)}) copy-start(bf16[2048,768]{1,0:T(8,128)(2,1)} %param.11) | copy-start | bytes 9437188
  7.2 120.9 %all-gather.11.cloned.1.call-start = ((), (), s32[]{:S(2)}) async-start(), calls=%async_computation.4 | async-start | bytes 34603008 | tf_op jit(solution)/shard_map/all_gather | solution.py:64
  201.0 12.6 %all-to-all-start = ((f32[32,1,256]{2,1,0:T(1,128)}), f32[32,1,256]{2,1,0:T(1,128)S(1)}, u32[]{:S(2)}, u32[]{:S(2)}) async-start(f32[32,1,256]{2,1,0:T(1,128)} %all_to_all.30), calls=%async_computation | async-start | bytes 65536 | tf_op jit(solution)/shard_map/all_to_all | solution.py:70
  213.6 11.3 %all-to-all-start.1 = ((f32[32,1,256]{2,1,0:T(1,128)}), f32[32,1,256]{2,1,0:T(1,128)S(1)}, u32[]{:S(2)}, u32[]{:S(2)}) async-start(f32[32,1,256]{2,1,0:T(1,128)} %all_to_all.32), calls=%async_computation.1 | async-start | bytes 65536 | tf_op jit(solution)/shard_map/all_to_all | solution.py:71
  224.9 11.3 %all-to-all-start.2 = ((f32[32,1,256]{2,1,0:T(1,128)}), f32[32,1,256]{2,1,0:T(1,128)S(1)}, u32[]{:S(2)}, u32[]{:S(2)}) async-start(f32[32,1,256]{2,1,0:T(1,128)} %all_to_all.36), calls=%async_computation.2 | async-start | bytes 65536 | tf_op jit(solution)/shard_map/all_to_all | solution.py:72
  236.2 29.5 %all-to-all-start.3 = ((f32[32,1,256]{2,1,0:T(1,128)}), f32[32,1,256]{2,1,0:T(1,128)S(1)}, u32[]{:S(2)}, u32[]{:S(2)}) async-start(f32[32,1,256]{2,1,0:T(1,128)} %all_to_all.39), calls=%async_computation.3 | async-start | bytes 65536 | tf_op jit(solution)/shard_map/all_to_all | solution.py:73
Sparse Core Ops, SparseCore 0:
  11.6 116.4 all-gather.10
where the time goes:
time: 284 us; the launch traced here: 283 us
  waiting for transfers between devices  111 us (39%)
  blocking collectives  58.2 us (20%)
  matrix products  55.4 us (20%)
  other arithmetic  17.6 us (6%)
  starting transfers between devices  16.7 us (6%)
  between operations  16.6 us (6%)
  local copies, waits for them, and re-layouts  6.78 us (2%)
    all_gather x1, waiting for transfers between devices, per_device(): block = lax.all_gather(normed, 'req', axis=0, tiled=True)  90.9 us
    dot_general x16, matrix products, block_stats(): logits = jnp.dot(block, matrix, preferred_element_type=jnp.float32)  55.4 us
    all_gather x4, blocking collectives, combined_all(): everything = jax.tree.map(lambda part: lax.all_gather(part, axis), value)  32.6 us
    all_gather x1, blocking collectives, per_device(): target = lax.all_gather(target_ids, 'req', axis=0, tiled=True)  25.6 us
    reduce_sum x16, other arithmetic, block_stats(): weighted = jnp.sum(shifted * logits, axis=-1)  11.5 us
    all_to_all x1, waiting for transfers between devices, per_device(): lax.all_to_all(shaped[1], 'req', split_axis=0, concat_axis=0, tiled=True)  6.79 us
    all_to_all x1, waiting for transfers between devices, per_device(): lax.all_to_all(shaped[0], 'req', split_axis=0, concat_axis=0, tiled=True)  6.79 us
    all_to_all x1, waiting for transfers between devices, per_device(): lax.all_to_all(shaped[2], 'req', split_axis=0, concat_axis=0, tiled=True)  6.09 us
  transfers between devices with their start and end apart: 5, of which 4 were waited for; matrix products, arithmetic and copies ran while one was open for 0% of the time, Pallas kernels for 0%

commit v1 on v0

v1 whole, which is shorter than its diff:
```python
import jax
import jax.numpy as jnp
from jax import lax
from jax.sharding import PartitionSpec as P

CHUNKS = 4


def chunk_stats(block, target, matrix, vocab_ids):
    logits = jnp.dot(block, matrix, preferred_element_type=jnp.float32)
    top = jnp.max(logits, axis=-1)
    shifted = jnp.exp(logits - top[:, None])
    weight_sum = jnp.sum(shifted, axis=-1)
    weighted = jnp.sum(shifted * logits, axis=-1)
    hit = vocab_ids == target[:, None]
    picked = jnp.sum(jnp.where(hit, logits, 0.0), axis=-1)
    return jnp.stack([top, weight_sum, weighted, picked])


def merge(stats, axis):
    top = jnp.max(stats[:, 0], axis=axis)
    factor = jnp.exp(stats[:, 0] - jnp.expand_dims(top, axis))
    return (
        top,
        jnp.sum(stats[:, 1] * factor, axis=axis),
        jnp.sum(stats[:, 2] * factor, axis=axis),
        jnp.sum(stats[:, 3], axis=axis),
    )


def per_device(hidden_states, norm_gain, head, target_ids, lengths):
    feats = hidden_states.astype(jnp.float32)
    scale = lax.rsqrt(jnp.mean(feats * feats, axis=-1, keepdims=True) + 1e-06)
    normed = (feats * scale * norm_gain).astype(jnp.bfloat16)
    rows = hidden_states.shape[0]
    vdev = head.shape[1]
    n_req = lax.axis_size("req")
    n_tp = lax.axis_size("tp")
    vbase = (lax.axis_index("req") * n_tp + lax.axis_index("tp")) * vdev
    own_vocab = lax.broadcasted_iota(jnp.int32, (1, vdev), 1) + vbase
    step = rows // CHUNKS
    digits = jnp.concatenate([target_ids % 64, (target_ids // 64) % 64, target_ids // 4096])
    extra = jnp.zeros((16, normed.shape[1]), jnp.bfloat16)
    extra = extra.at[0, : 3 * rows].set(digits.astype(jnp.bfloat16))
    parts = []
    targets = None
    for c in range(CHUNKS):
        piece = normed[c * step:(c + 1) * step]
        if c == 0:
            piece = jnp.concatenate([piece, extra], axis=0)
        block = lax.all_gather(piece, "req", axis=0, tiled=False)
        if c == 0:
            code = block[:, step, : 3 * rows].astype(jnp.int32).reshape(n_req, 3, rows)
            targets = code[:, 0] + code[:, 1] * 64 + code[:, 2] * 4096
            block = block[:, :step]
        target = targets[:, c * step:(c + 1) * step].reshape(-1)
        st = chunk_stats(block.reshape(-1, block.shape[2]), target, head, own_vocab)
        parts.append(st.reshape(4, n_req, step))
    stats = jnp.concatenate(parts, axis=2)
    arrived = lax.all_to_all(stats, "req", split_axis=1, concat_axis=1, tiled=True)
    own = merge(jnp.moveaxis(arrived, 1, 0), axis=0)
    own = jnp.stack(own)
    everyone = lax.all_gather(own, "tp", axis=0)
    top, weight_sum, weighted, picked = merge(everyone, axis=0)
    log_norm = top + jnp.log(weight_sum)
    live = jnp.arange(rows, dtype=jnp.int32) < lengths[0]
    logprob = jnp.where(live, picked - log_norm, jnp.float32(0.0))
    entropy = jnp.where(live, log_norm - weighted / weight_sum, jnp.float32(0.0))
    mean_lp = (jnp.sum(logprob) / lengths[0].astype(jnp.float32)).reshape(1)
    top_live = jnp.max(jnp.where(live, top, jnp.float32(-1e30))).reshape(1)
    return (logprob, entropy, mean_lp, top_live)


def solution(mesh):
    in_specs = (P("req", None), P(), P(None, ("req", "tp")), P("req"), P("req"))
    out_specs = (P("req"), P("req"), P("req"), P("req"))
    return jax.shard_map(
        per_device, mesh=mesh, in_specs=in_specs, out_specs=out_specs, check_vma=False
    )
```

time: 284 us -> 307 us (1.081)
  waiting for transfers between devices: 111 us -> 198 us
  blocking collectives: 58.2 us -> 12.3 us
  matrix products: 55.4 us -> 43.3 us
  starting transfers between devices: 16.7 us -> 5.6 us
  local copies, waits for them, and re-layouts: 6.78 us -> 12.1 us
    all_gather x1 -> x4, waiting for transfers between devices: 90.9 us -> 189 us  [per_device(): block = lax.all_gather(piece, 'req', axis=0, tiled=False)]
    all_gather x5 -> x1, blocking collectives: 58.2 us -> 12.3 us  [per_device(): everyone = lax.all_gather(own, 'tp', axis=0)]
    all_to_all x4 -> x1, waiting for transfers between devices: 19.7 us -> 7.21 us  [per_device(): lax.all_to_all(stats, 'req', split_axis=1, concat_axis=1, tiled=True)]
    dot_general x16 -> x4, matrix products: 55.4 us -> 43.3 us  [chunk_stats(): logits = jnp.dot(block, matrix, preferred_element_type=jnp.float32)]
    all_to_all x4 -> x1, starting transfers between devices: 16.7 us -> 5.44 us  [per_device(): lax.all_to_all(stats, 'req', split_axis=1, concat_axis=1, tiled=True)]
    slice x4, local copies, waits for them, and re-layouts: 0.01 us -> 10.4 us  [the longest x1 8.39 us: per_device(): block = block[:, :step]]
    dynamic_update_slice x64 -> x0, local copies, waits for them, and re-layouts: 3.97 us -> none  [blocked_stats(): lax.map(lambda a: block_stats(a[0], a[1], matrix, vocab_ids), (block.resh...]
    reduce_sum x18 -> x3, other arithmetic: 11.6 us -> 12 us  [the longest x1 12 us: chunk_stats(): weight_sum = jnp.sum(shifted, axis=-1)]
  transfers between devices with their start and end apart: 5 -> 5, of which waited for: 4 -> 5; matrix products, arithmetic and copies ran while one was open for 0% -> 11% of each run, Pallas kernels for 0% -> 0%
where the time goes in v1:
time: 307 us
  waiting for transfers between devices  198 us (64%)
  matrix products  43.3 us (14%)
  other arithmetic  19.3 us (6%)
  between operations  16.4 us (5%)
  blocking collectives  12.3 us (4%)
  local copies, waits for them, and re-layouts  12.1 us (4%)
  starting transfers between devices  5.6 us (2%)
    all_gather x4, waiting for transfers between devices, per_device(): block = lax.all_gather(piece, 'req', axis=0, tiled=False)  189 us
    dot_general x4, matrix products, chunk_stats(): logits = jnp.dot(block, matrix, preferred_element_type=jnp.float32)  43.3 us
    all_gather x1, blocking collectives, per_device(): everyone = lax.all_gather(own, 'tp', axis=0)  12.3 us
    reduce_sum x1, other arithmetic, chunk_stats(): weight_sum = jnp.sum(shifted, axis=-1)  12 us
    slice x1, local copies, waits for them, and re-layouts, per_device(): block = block[:, :step]  8.39 us
    all_to_all x1, waiting for transfers between devices, per_device(): lax.all_to_all(stats, 'req', split_axis=1, concat_axis=1, tiled=True)  7.21 us
  transfers between devices with their start and end apart: 5, of which 5 were waited for; matrix products, arithmetic and copies ran while one was open for 11% of the time, Pallas kernels for 0%

profile of v1, /device:TPU:0, one launch (start us, length us, event | category | flops | bytes accessed | tf_op | source)
XLA Modules:
  0.0 306.7 jit_solution(13360459740497236305)
XLA Ops:
  7.2 1.7 fusion.4
  8.9 1.5 fusion.6
  10.4 0.9 fusion.33
  11.4 0.7 all-gather.15.cloned.1.call-update
  12.2 0.7 all-gather.17.cloned.1.call-update
  12.9 0.7 fusion.29
  13.7 0.8 pad_maximum_fusion
  14.5 52.5 %all-gather.13.cloned.1.call-done = bf16[2048,2048]{1,0:T(8,128)(2,1)} async-done(((bf16[64,2048]{1,0:T(8,128)(2,1)}), bf16[2048,2048]{1,0:T(8,128)(2,1)}) %all-gather.13.cloned.1.call-update) | async-done | bytes 8388624 | tf_op jit(solution)/shard_map/all_gather | solution.py:51
  67.0 10.8 %fusion.38 = (f32[2048]{0:T(1024)S(1)}, f32[2048,768]{0,1:T(8,128)}) fusion(bf16[2048,2048]{1,0:T(8,128)(2,1)} %all-gather.13.cloned.1.call-done, bf16[2048,768]{1,0:T(8,128)(2,1)S(1)} %copy-done), kind=kOutput, calls=%fused_computation.92 | convolution fusion | flops 6444021760 | bytes 17833984 | tf_op jit(solution)/shard_map/dot_general | solution.py:10
  77.9 43.9 %all-gather.15.cloned.1.call-done = bf16[2048,2048]{1,0:T(8,128)(2,1)} async-done(((bf16[64,2048]{1,0:T(8,128)(2,1)}), bf16[2048,2048]{1,0:T(8,128)(2,1)}) %all-gather.15.cloned.1.call-update) | async-done | bytes 8388624 | tf_op jit(solution)/shard_map/all_gather | solution.py:51
  121.8 10.8 %fusion.39 = (f32[2048]{0:T(1024)S(1)}, f32[2048,768]{0,1:T(8,128)}) fusion(bf16[2048,2048]{1,0:T(8,128)(2,1)} %all-gather.15.cloned.1.call-done, bf16[2048,768]{1,0:T(8,128)(2,1)S(1)} %copy-done), kind=kOutput, calls=%fused_computation.93 | convolution fusion | flops 6444021760 | bytes 17833984 | tf_op jit(solution)/shard_map/dot_general | solution.py:10
  132.7 44.0 %all-gather.17.cloned.1.call-done = bf16[2048,2048]{1,0:T(8,128)(2,1)} async-done(((bf16[64,2048]{1,0:T(8,128)(2,1)}), bf16[2048,2048]{1,0:T(8,128)(2,1)}) %all-gather.17.cloned.1.call-update) | async-done | bytes 8388624 | tf_op jit(solution)/shard_map/all_gather | solution.py:51
  176.7 10.8 %fusion.40 = (f32[2048]{0:T(1024)S(1)}, f32[2048,768]{0,1:T(8,128)}) fusion(bf16[2048,2048]{1,0:T(8,128)(2,1)} %all-gather.17.cloned.1.call-done, bf16[2048,768]{1,0:T(8,128)(2,1)S(1)} %copy-done), kind=kOutput, calls=%fused_computation.94 | convolution fusion | flops 6444021760 | bytes 17833984 | tf_op jit(solution)/shard_map/dot_general | solution.py:10
  187.5 48.7 %all-gather.11.cloned.1.call-done = bf16[2560,2048]{1,0:T(8,128)(2,1)} async-done(((bf16[80,2048]{1,0:T(8,128)(2,1)}), bf16[2560,2048]{1,0:T(8,128)(2,1)}) %all-gather.11.cloned.1.call-update) | async-done | bytes 10485776 | tf_op jit(solution)/shard_map/all_gather | solution.py:51
  236.2 1.0 slice.104
  237.3 8.4 %slice.103 = bf16[32,64,2048]{2,1,0:T(8,128)(2,1)} slice(bf16[32,80,2048]{2,1,0:T(8,128)(2,1)} %bitcast.69), slice={[0:32], [0:64], [0:2048]} | slice | bytes 16777216 | tf_op jit(solution)/shard_map/slice | solution.py:55
  246.2 10.9 %fusion.37 = (f32[2048]{0:T(1024)S(1)}, f32[2048,768]{0,1:T(8,128)}) fusion(bf16[2048,2048]{1,0:T(8,128)(2,1)} %bitcast.67, bf16[2048,768]{1,0:T(8,128)(2,1)S(1)} %copy-done), kind=kOutput, calls=%fused_computation.91 | convolution fusion | flops 6444021760 | bytes 17833984 | tf_op jit(solution)/shard_map/dot_general | solution.py:10
  257.2 12.0 %fusion.3 = (f32[2048]{0:T(1024)S(1)}, f32[2048]{0:T(1024)S(1)}, f32[2048]{0:T(1024)S(1)}, f32[2048]{0:T(1024)S(1)}, f32[2048]{0:T(1024)S(1)}, /*index=5*/f32[20...) fusion(f32[2048,768]{0,1:T(8,128)} %get-tuple-element.71, ...), kind=kLoop, calls=%fused_computation.15 | loop fusion | flops 44015616 | bytes 25332736 | tf_op jit(solution)/shard_map/reduce_sum | solution.py:13
  270.1 1.1 maximum_maximum_fusion
  271.3 5.4 %all-to-all-start = ((f32[4,32,256]{2,0,1:T(4,128)}), f32[4,32,256]{2,0,1:T(4,128)S(1)}, u32[]{:S(2)}, u32[]{:S(2)}) async-start(f32[4,32,256]{2,0,1:T(4,128)} %maximum_maximum_fusion), calls=%async_computation | async-start | bytes 262144 | tf_op jit(solution)/shard_map/all_to_all | solution.py:60
  277.4 7.2 %all-to-all-done = f32[4,32,256]{2,0,1:T(4,128)S(1)} async-done(((f32[4,32,256]{2,0,1:T(4,128)}), f32[4,32,256]{2,0,1:T(4,128)S(1)}, u32[]{:S(2)}, u32[]{:S(2)}) %all-to-all-start) | async-done | bytes 131104 | tf_op jit(solution)/shard_map/all_to_all | solution.py:60
  284.6 0.1 fusion.34
  284.7 12.3 %all-gather.5 = f32[4,4,256]{2,1,0:T(4,128)S(1)} all-gather(f32[1,4,256]{2,1,0:T(4,128)S(1)} %maximum_bitcast_fusion), channel_id=6, replica_groups=mesh['req'=32,'tp'=4] {'tp'}, dimensions={0}, use_global_device_ids=true | all-gather | bytes 20480 | tf_op jit(solution)/shard_map/all_gather | solution.py:63
  297.1 1.3 fusion.32
  (43 shorter events, 2.1 us)
Async XLA Ops:
  7.2 59.9 %copy-start = (bf16[2048,768]{1,0:T(8,128)(2,1)S(1)}, bf16[2048,768]{1,0:T(8,128)(2,1)}, u32[]{:S(2)}) copy-start(bf16[2048,768]{1,0:T(8,128)(2,1)} %param.9) | copy-start | bytes 9437188
  7.2 59.9 %all-gather.13.cloned.1.call-start = ((), (), s32[]{:S(2)}) async-start(), calls=%async_computation.2 | async-start | bytes 8650752 | tf_op jit(solution)/shard_map/all_gather | solution.py:51
  11.4 110.5 %all-gather.15.cloned.1.call-start = ((), (), s32[]{:S(2)}) async-start(), calls=%async_computation.3 | async-start | bytes 8650752 | tf_op jit(solution)/shard_map/all_gather | solution.py:51
  12.1 164.5 %all-gather.17.cloned.1.call-start = ((), (), s32[]{:S(2)}) async-start(), calls=%async_computation.4 | async-start | bytes 8650752 | tf_op jit(solution)/shard_map/all_gather | solution.py:51
  12.9 223.4 %all-gather.11.cloned.1.call-start = ((), (), s32[]{:S(2)}) async-start(), calls=%async_computation.1 | async-start | bytes 10813440 | tf_op jit(solution)/shard_map/all_gather | solution.py:51
  271.3 13.3 %all-to-all-start = ((f32[4,32,256]{2,0,1:T(4,128)}), f32[4,32,256]{2,0,1:T(4,128)S(1)}, u32[]{:S(2)}, u32[]{:S(2)}) async-start(f32[4,32,256]{2,0,1:T(4,128)} %maximum_maximum_fusion), calls=%async_computation | async-start | bytes 262144 | tf_op jit(solution)/shard_map/all_to_all | solution.py:60
Sparse Core Ops, SparseCore 0:
  11.5 55.4 all-gather.12
  69.3 52.5 all-gather.14
  124.1 52.5 all-gather.16
  178.8 57.4 all-gather.10

commit v2 on v1

v2 whole, which is shorter than its diff:
```python
import jax
import jax.numpy as jnp
import numpy as np
from jax import lax
from jax.experimental import pallas as pl
from jax.experimental.pallas import tpu as pltpu
from jax.sharding import Mesh, PartitionSpec as P

MESH = pl.DeviceIdType.MESH
PAD = 16


def swap_kernel(src_ref, dst_ref, send_sem, recv_sem):
    chip = lax.axis_index("chip")
    other = 1 - lax.axis_index("core")
    tp = lax.axis_index("tp")
    barrier = pltpu.get_barrier_semaphore()
    pl.semaphore_signal(barrier, inc=1, device_id=(chip, other, tp), device_id_type=MESH)
    pl.semaphore_wait(barrier, 1)
    copy = pltpu.make_async_remote_copy(
        src_ref=src_ref,
        dst_ref=dst_ref,
        send_sem=send_sem,
        recv_sem=recv_sem,
        device_id=(chip, other, tp),
        device_id_type=MESH,
    )
    copy.start()
    copy.wait()


def swap_with_other_core(head):
    return pl.pallas_call(
        swap_kernel,
        out_shape=jax.ShapeDtypeStruct(head.shape, head.dtype),
        in_specs=[pl.BlockSpec(memory_space=pl.ANY)],
        out_specs=pl.BlockSpec(memory_space=pl.ANY),
        scratch_shapes=[pltpu.SemaphoreType.DMA, pltpu.SemaphoreType.DMA],
        compiler_params=pltpu.CompilerParams(collective_id=0, has_side_effects=True),
    )(head)


def chunk_stats(block, target, matrix, vocab_ids):
    logits = jnp.dot(block, matrix, preferred_element_type=jnp.float32)
    top = jnp.max(logits, axis=-1)
    shifted = jnp.exp(logits - top[:, None])
    weight_sum = jnp.sum(shifted, axis=-1)
    weighted = jnp.sum(shifted * logits, axis=-1)
    hit = vocab_ids == target[:, None]
    picked = jnp.sum(jnp.where(hit, logits, 0.0), axis=-1)
    return jnp.stack([top, weight_sum, weighted, picked])


def merge(stats, axis):
    top = jnp.max(stats[:, 0], axis=axis)
    factor = jnp.exp(stats[:, 0] - jnp.expand_dims(top, axis))
    return (
        top,
        jnp.sum(stats[:, 1] * factor, axis=axis),
        jnp.sum(stats[:, 2] * factor, axis=axis),
        jnp.sum(stats[:, 3], axis=axis),
    )


def per_device(hidden_states, norm_gain, head, target_ids, lengths):
    feats = hidden_states.astype(jnp.float32)
    scale = lax.rsqrt(jnp.mean(feats * feats, axis=-1, keepdims=True) + 1e-06)
    normed = (feats * scale * norm_gain).astype(jnp.bfloat16)
    rows = hidden_states.shape[0]
    vdev = head.shape[1]
    n_chip = lax.axis_size("chip")
    n_tp = lax.axis_size("tp")
    chip = lax.axis_index("chip")
    core = lax.axis_index("core")
    tp = lax.axis_index("tp")
    digits = jnp.concatenate([target_ids % 64, (target_ids // 64) % 64, target_ids // 4096])
    extra = jnp.zeros((PAD, normed.shape[1]), jnp.bfloat16)
    extra = extra.at[0, : 3 * rows].set(digits.astype(jnp.bfloat16))
    piece = jnp.concatenate([normed, extra], axis=0)
    other_head = swap_with_other_core(head)
    block = lax.all_gather(piece, "chip", axis=0, tiled=False)
    code = block[:, rows, : 3 * rows].astype(jnp.int32).reshape(n_chip, 3, rows)
    targets = code[:, 0] + code[:, 1] * 64 + code[:, 2] * 4096
    targets = jnp.pad(targets, ((0, 0), (0, PAD)), constant_values=-1).reshape(-1)
    flat = block.reshape(-1, block.shape[2])
    columns = lax.broadcasted_iota(jnp.int32, (1, vdev), 1)
    own_base = ((chip * 2 + core) * n_tp + tp) * vdev
    other_base = ((chip * 2 + 1 - core) * n_tp + tp) * vdev
    s_own = chunk_stats(flat, targets, head, columns + own_base)
    s_other = chunk_stats(flat, targets, other_head, columns + other_base)
    first = jnp.where(core == 0, s_own, s_other)
    second = jnp.where(core == 0, s_other, s_own)
    pair = jnp.stack([first, second])
    stats = jnp.stack(merge(pair, axis=0)).reshape(4, n_chip, rows + PAD)[:, :, :rows]
    arrived = lax.all_to_all(stats, "chip", split_axis=1, concat_axis=1, tiled=True)
    own = jnp.stack(merge(jnp.moveaxis(arrived, 1, 0), axis=0))
    everyone = lax.all_gather(own, "tp", axis=0)
    top, weight_sum, weighted, picked = merge(everyone, axis=0)
    log_norm = top + jnp.log(weight_sum)
    live = jnp.arange(rows, dtype=jnp.int32) < lengths[0]
    logprob = jnp.where(live, picked - log_norm, jnp.float32(0.0))
    entropy = jnp.where(live, log_norm - weighted / weight_sum, jnp.float32(0.0))
    mean_lp = (jnp.sum(logprob) / lengths[0].astype(jnp.float32)).reshape(1)
    top_live = jnp.max(jnp.where(live, top, jnp.float32(-1e30))).reshape(1)
    return (logprob, entropy, mean_lp, top_live)


def solution(mesh):
    n_req, n_tp = mesh.devices.shape
    devices = np.asarray(mesh.devices).reshape(n_req // 2, 2, n_tp)
    fine = Mesh(devices, ("chip", "core", "tp"))
    rq = ("chip", "core")
    in_specs = (P(rq, None), P(), P(None, (*rq, "tp")), P(rq), P(rq))
    out_specs = (P(rq), P(rq), P(rq), P(rq))
    return jax.shard_map(
        per_device, mesh=fine, in_specs=in_specs, out_specs=out_specs, check_vma=False
    )
```

time: 307 us -> 224 us (0.73)
  waiting for transfers between devices: 198 us -> 120 us
  local copies, waits for them, and re-layouts: 12.1 us -> 1.64 us
  Pallas kernels: 0 us -> 6.1 us
    all_gather x4 -> x1, waiting for transfers between devices: 189 us -> 113 us  [per_device(): block = lax.all_gather(piece, 'chip', axis=0, tiled=False)]
    slice x4 -> x1, local copies, waits for them, and re-layouts: 10.4 us -> 0.95 us  [per_device(): code = block[:, rows, :3 * rows].astype(jnp.int32).reshape(n_chip, 3, rows)]
    pallas_call x0 -> x1, Pallas kernels: none -> 6.1 us  [swap_with_other_core(): pl.pallas_call(swap_kernel, out_shape=jax.ShapeDtypeStruct(head.shape, he...]
    dot_general x4 -> x2, matrix products: 43.3 us -> 41.4 us  [chunk_stats(): logits = jnp.dot(block, matrix, preferred_element_type=jnp.float32)]
  transfers between devices with their start and end apart: 5 -> 2, of which waited for: 5 -> 2; matrix products, arithmetic and copies ran while one was open for 11% -> 0% of each run, Pallas kernels for 0% -> 3%
where the time goes in v2:
time: 224 us
  waiting for transfers between devices  120 us (54%)
  matrix products  41.4 us (18%)
  other arithmetic  20.3 us (9%)
  between operations  16.7 us (7%)
  blocking collectives  12.3 us (5%)
  Pallas kernels  6.1 us (3%)
  starting transfers between devices  5.34 us (2%)
    all_gather x1, waiting for transfers between devices, per_device(): block = lax.all_gather(piece, 'chip', axis=0, tiled=False)  113 us
    dot_general x2, matrix products, chunk_stats(): logits = jnp.dot(block, matrix, preferred_element_type=jnp.float32)  41.4 us
    reduce_sum x1, other arithmetic, chunk_stats(): weighted = jnp.sum(shifted * logits, axis=-1)  12.8 us
    all_gather x1, blocking collectives, per_device(): everyone = lax.all_gather(own, 'tp', axis=0)  12.3 us
    all_to_all x1, waiting for transfers between devices, per_device(): lax.all_to_all(stats, 'chip', split_axis=1, concat_axis=1, tiled=True)  7.02 us
    pallas_call x1, Pallas kernels, swap_with_other_core(): pl.pallas_call(swap_kernel, out_shape=jax.ShapeDtypeStruct(head.shape, he...  6.1 us
    all_to_all x1, starting transfers between devices, per_device(): lax.all_to_all(stats, 'chip', split_axis=1, concat_axis=1, tiled=True)  5.3 us
  transfers between devices with their start and end apart: 2, of which 2 were waited for; matrix products, arithmetic and copies ran while one was open for 0% of the time, Pallas kernels for 3%

profile of v2, /device:TPU:0, one launch (start us, length us, event | category | flops | bytes accessed | tf_op | source)
XLA Modules:
  0.0 224.0 jit_solution(4356836568247112101)
XLA Ops:
  7.2 1.5 fusion.2
  8.7 0.7 fusion.34
  9.5 1.5 fusion.4
  11.0 1.1 pad_maximum_fusion
  12.2 6.1 %shard_map.84 = bf16[2048,768]{1,0:T(8,128)(2,1)} custom-call(bf16[2048,768]{1,0:T(8,128)(2,1)} %src_ref.1), custom_call_target="tpu_custom_call" | custom-call | tf_op jit(solution)/shard_map/pallas_call | solution.py:33
  18.3 113.3 %all-gather.5.cloned.1.call-done = bf16[4352,2048]{1,0:T(8,128)(2,1)} async-done(((bf16[272,2048]{1,0:T(8,128)(2,1)}), bf16[4352,2048]{1,0:T(8,128)(2,1)}) %all-gather.5.cloned.1.call-update) | async-done | bytes 17825808 | tf_op jit(solution)/shard_map/all_gather | solution.py:81
  131.6 1.0 slice.87
  132.7 0.1 eq.35
  132.8 21.3 %fusion.43 = (f32[4352]{0:T(1024)S(1)}, f32[4352,768]{0,1:T(8,128)}) fusion(bf16[4352,2048]{1,0:T(8,128)(2,1)} %all-gather.5.cloned.1.call-done, bf16[2048,768]{1,0:T(8,128)(2,1)} %shard_map.84), kind=kOutput, calls=%fused_computation.113 | convolution fusion | flops 13693546496 | bytes 34358272 | tf_op jit(solution)/shard_map/dot_general | solution.py:44
  154.0 20.1 %fusion.42 = (f32[4352]{0:T(1024)S(1)}, f32[4352,768]{0,1:T(8,128)}) fusion(bf16[4352,2048]{1,0:T(8,128)(2,1)} %all-gather.5.cloned.1.call-done, bf16[2048,768]{1,0:T(8,128)(2,1)S(1)} %copy-done), kind=kOutput, calls=%fused_computation.112 | convolution fusion | flops 13693546496 | bytes 34358272 | tf_op jit(solution)/shard_map/dot_general | solution.py:44
  174.2 12.8 %multiply_reduce_fusion.1 = (f32[4352]{0:T(1024)S(1)}, f32[4352]{0:T(1024)S(1)}, f32[4352]{0:T(1024)S(1)}, f32[4352]{0:T(1024)S(1)}, f32[4352]{0:T(1024)S(1)}, /*index=5*/f32[4352]{0:T(1024)S(1)}) fusion(f32[4352,768]{0,1:T(8,128)} %get-tuple-element.58, f32[4352]{0:T(1024)S(1)} %get-tuple-element.57, s32[4352]{0:T(1024)S(1)} %eq.35, ...), kind=kLoop, calls=%fused_computation.5 | loop fusion | flops 46766592 | bytes 26901504 | tf_op jit(solution)/shard_map/reduce_sum | solution.py:48
  187.1 0.1 broadcast_select_fusion.1
  187.2 0.1 fusion.38
  187.4 0.1 stack.76
  187.5 0.2 fusion.20
  187.6 0.1 stack.77
  187.8 0.1 stack.78
  187.9 0.1 stack.79
  188.0 0.7 pad_maximum_fusion.1
  188.7 5.3 %all-to-all-start = ((f32[4,16,256]{2,0,1:T(4,128)}), f32[4,16,256]{2,0,1:T(4,128)S(1)}, u32[]{:S(2)}, u32[]{:S(2)}) async-start(f32[4,16,256]{2,0,1:T(4,128)} %pad_maximum_fusion.1), calls=%async_computation | async-start | bytes 131072 | tf_op jit(solution)/shard_map/all_to_all | solution.py:95
  194.6 7.0 %all-to-all-done = f32[4,16,256]{2,0,1:T(4,128)S(1)} async-done(((f32[4,16,256]{2,0,1:T(4,128)}), f32[4,16,256]{2,0,1:T(4,128)S(1)}, u32[]{:S(2)}, u32[]{:S(2)}) %all-to-all-start) | async-done | bytes 65568 | tf_op jit(solution)/shard_map/all_to_all | solution.py:95
  201.6 0.1 fusion.40
  201.7 12.3 %all-gather.2 = f32[4,4,256]{2,1,0:T(4,128)S(1)} all-gather(f32[1,4,256]{2,1,0:T(4,128)S(1)} %maximum_bitcast_fusion), channel_id=3, replica_groups=mesh['chip'=16,'core'=2,'tp'=4] {'tp'}, dimensions={0}, use_global_device_ids=true | all-gather | bytes 20480 | tf_op jit(solution)/shard_map/all_gather | solution.py:97
  214.1 1.3 fusion.37
  (27 shorter events, 0.4 us)
Async XLA Ops:
  7.2 124.4 %all-gather.5.cloned.1.call-start = ((), (), s32[]{:S(2)}) async-start(), calls=%async_computation.1 | async-start | bytes 18939904 | tf_op jit(solution)/shard_map/all_gather | solution.py:81
  132.7 21.3 %copy-start = (bf16[2048,768]{1,0:T(8,128)(2,1)S(1)}, bf16[2048,768]{1,0:T(8,128)(2,1)}, u32[]{:S(2)}) copy-start(bf16[2048,768]{1,0:T(8,128)(2,1)} %src_ref.1) | copy-start | bytes 9437188
  188.7 13.0 %all-to-all-start = ((f32[4,16,256]{2,0,1:T(4,128)}), f32[4,16,256]{2,0,1:T(4,128)S(1)}, u32[]{:S(2)}, u32[]{:S(2)}) async-start(f32[4,16,256]{2,0,1:T(4,128)} %pad_maximum_fusion.1), calls=%async_computation | async-start | bytes 131072 | tf_op jit(solution)/shard_map/all_to_all | solution.py:95
Sparse Core Ops, SparseCore 0:
  12.3 119.2 all-gather.4
